TPU v7x, 512 devices: a whole 4x8x8 slice. The times are simulated.
512 devices in a mesh: dp: 64 (over y, x, core), space: 8 (over z).
Axes of the slice: x: 4, y: 8, z: 8, core: 2. Of those that a mesh axis runs over, the one named last changes fastest.
Arguments:
- image: bfloat16 [64, 32, 8, 8, 128], P('dp', 'space'), may hold values from -30 to 30
- cotangent: bfloat16 [64, 32, 8, 8, 128], P('dp', 'space'), may hold values from -30 to 30
- first_weight: bfloat16 [3456, 128], P('dp'), may hold values from -0.109375 to 0.109375
- second_weight: bfloat16 [3456, 128], P('dp'), may hold values from -0.109375 to 0.109375
Outputs:
- output: bfloat16 [64, 32, 8, 8, 128], P('dp', 'space')
- image_grad: bfloat16 [64, 32, 8, 8, 128], P('dp', 'space')
- first_grad: float32 [3456, 128], P('dp')
- second_grad: float32 [3456, 128], P('dp')
All inputs are finite; a program needn't handle non-finite values.
Results may differ from a plain program's by a relative error of at most 0.013.
Values may be sent and summed in bfloat16 or wider, within the bound.
No kernel may reach another device: no remote copies, remote signals or barrier semaphores. Data moves between devices by JAX's collectives and lax.ppermute only.
A program may use at most 64 MiB of HBM per device.

v0:
```python
import math

import jax
import jax.numpy as jnp
from jax import lax
from jax.sharding import PartitionSpec as P

EPSILON = 1e-05


def with_halo(cells, sides, width):
    for axis, dim in sides:
        count = lax.axis_size(axis)
        ends = count - 1
        head = lax.slice_in_dim(cells, 0, width, axis=dim)
        tail = lax.slice_in_dim(cells, cells.shape[dim] - width, cells.shape[dim], axis=dim)
        cells = jnp.concatenate(
            [
                lax.ppermute(tail, axis, [(i, (i + 1) % count) for i in range(ends)]),
                cells,
                lax.ppermute(head, axis, [((i + 1) % count, i) for i in range(ends)]),
            ],
            axis=dim,
        )
    return cells


def gelu_value(values):
    return 0.5 * values * (1.0 + lax.erf(values * 0.7071067811865476))


def gelu_slope(values):
    return (
        0.5 * (1.0 + lax.erf(values * 0.7071067811865476))
        + values * jnp.exp(-0.5 * values * values) * 0.3989422804014327
    )


def columns(deep):
    depth = deep.shape[0] - 2
    height, width, channels = (deep.shape[1], deep.shape[2], deep.shape[3])
    padded = jnp.pad(deep, ((0, 0), (1, 1), (1, 1), (0, 0)))
    pieces = [
        padded[first : first + depth, second : second + height, third : third + width, :]
        for first in range(3)
        for second in range(3)
        for third in range(3)
    ]
    return jnp.concatenate(pieces, axis=-1).reshape(depth * height * width, 27 * channels)


def reverse_taps(weight):
    channels = weight.shape[1]
    return (
        weight.reshape(27, channels, channels)[::-1]
        .transpose(0, 2, 1)
        .reshape(27 * channels, channels)
    )


def body(image, cotangent, first_weight, second_weight):
    slab = image[0]
    depth, height, width, channels = slab.shape
    cells = depth * height * width
    patch_cells = cells * lax.axis_size("space")
    factor = 1.0 / math.sqrt(patch_cells * lax.axis_size("dp"))

    def unfold_slab(volume):
        deep = with_halo(volume, (("space", 0),), 1)
        return columns(deep)

    def normalize(values):
        totals, squares = lax.psum(
            (jnp.sum(values, axis=0), jnp.sum(values * values, axis=0)), "space"
        )
        average = totals / patch_cells
        inverse = lax.rsqrt(squares / patch_cells - average * average + EPSILON)
        return ((values - average) * inverse, inverse)

    def norm_back(grad, normed, inverse):
        plain_total, paired_total = lax.psum(
            (jnp.sum(grad, axis=0), jnp.sum(grad * normed, axis=0)), "space"
        )
        return inverse * (grad - plain_total / patch_cells - normed * (paired_total / patch_cells))

    def apply_weight(unfolded, shard):
        whole = lax.all_gather(shard, "dp", axis=0, tiled=True)
        return (jnp.dot(unfolded, whole, preferred_element_type=jnp.float32), shard)

    def weight_again(kept):
        whole = lax.all_gather(kept, "dp", axis=0, tiled=True)
        return reverse_taps(whole)

    def reduce_grad(unfolded, delta):
        local = lax.dot_general(
            unfolded, delta, (((0,), (0,)), ((), ())), preferred_element_type=jnp.float32
        )
        summed_slabs = lax.psum(local.astype(jnp.bfloat16), "space").astype(jnp.float32)
        return lax.psum_scatter(summed_slabs, "dp", scatter_dimension=0, tiled=True)

    first_columns = unfold_slab(slab)
    first_conv, first_kept = apply_weight(first_columns, first_weight)
    first_norm, first_inverse = normalize(first_conv)
    hidden = gelu_value(first_norm).astype(jnp.bfloat16)
    second_columns = unfold_slab(hidden.reshape(depth, height, width, channels))
    second_conv, second_kept = apply_weight(second_columns, second_weight)
    second_norm, second_inverse = normalize(second_conv)
    summed = slab.reshape(cells, channels).astype(jnp.float32) + second_norm
    output = gelu_value(summed).astype(jnp.bfloat16)
    outer_grad = cotangent[0].reshape(cells, channels).astype(jnp.float32) * gelu_slope(summed)
    second_delta = norm_back(outer_grad, second_norm, second_inverse).astype(jnp.bfloat16)
    second_grad = reduce_grad(second_columns, second_delta)
    inner_grad = jnp.dot(
        unfold_slab(second_delta.reshape(depth, height, width, channels)),
        weight_again(second_kept),
        preferred_element_type=jnp.float32,
    )
    first_delta = norm_back(inner_grad * gelu_slope(first_norm), first_norm, first_inverse).astype(
        jnp.bfloat16
    )
    first_grad = reduce_grad(first_columns, first_delta)
    backward_term = jnp.dot(
        unfold_slab(first_delta.reshape(depth, height, width, channels)),
        weight_again(first_kept),
        preferred_element_type=jnp.float32,
    )
    image_grad = (outer_grad + backward_term).astype(jnp.bfloat16)
    return (
        output.reshape(image.shape),
        image_grad.reshape(image.shape),
        first_grad * factor,
        second_grad * factor,
    )


def solution(mesh):
    return jax.shard_map(
        body,
        mesh=mesh,
        in_specs=(
            P("dp", "space", None, None, None),
            P("dp", "space", None, None, None),
            P("dp", None),
            P("dp", None),
        ),
        out_specs=(
            P("dp", "space", None, None, None),
            P("dp", "space", None, None, None),
            P("dp", None),
            P("dp", None),
        ),
        check_vma=False,
    )
```

profile of v0, /device:TPU:8, one launch (start us, length us, event | category | flops | bytes accessed | tf_op | source)
XLA Modules:
  0.0 550.6 jit_solution(5301310722015317401)
XLA Ops:
  7.2 0.7 slice_bitcast_fusion.7
  8.0 4.3 collective-permute-start
  12.2 1.3 collective-permute-start.1
  13.5 50.6 %all-gather = bf16[64,54,128]{2,1,0:T(8,128)(2,1)S(1)} all-gather(bf16[1,54,128]{2,1,0:T(8,128)(2,1)} %bitcast.282), channel_id=1, replica_groups=mesh['dp'=64,'space'=8] {'dp'}, dimensions={0}, use_global_device_ids=true | all-gather | bytes 898560 | tf_op jit(solution)/shard_map/all_gather | solution.py:87
  64.2 1.2 reshape.175
  65.3 49.2 %all-gather.1 = bf16[64,54,128]{2,1,0:T(8,128)(2,1)S(1)} all-gather(bf16[1,54,128]{2,1,0:T(8,128)(2,1)S(1)} %bitcast.283), channel_id=1, replica_groups=mesh['dp'=64,'space'=8] {'dp'}, dimensions={0}, use_global_device_ids=true | all-gather | bytes 898560 | tf_op jit(solution)/shard_map/all_gather | solution.py:87
  114.6 2.2 reverse_bitcast_fusion
  116.8 1.1 reshape.180
  117.9 1.2 reshape.172
  121.3 23.5 %all-reduce.11 = (f32[128]{0:T(128)S(1)}, f32[128]{0:T(128)S(1)}) all-reduce(f32[128]{0:T(128)S(1)} %get-tuple-element.11, f32[128]{0:T(128)S(1)} %get-tuple-element.10), channel_id=1, replica_groups=mesh['dp'=64,'space'=8] {'space'}, use_global_device_ids=true, to_apply=%region_3.4 | all-reduce | flops 256 | bytes 2048 | tf_op jit(solution)/shard_map/psum | solution.py:73
  144.9 1.3 collective-permute-start.2
  146.2 1.3 collective-permute-start.3
  147.5 2.2 reverse_bitcast_fusion.1
  149.7 1.2 reshape.182
  150.8 2.3 copy.11
  153.1 1.6 copy.10
  154.8 1.3 dynamic-slice.6
  159.1 1.3 fusion.25
  160.3 17.1 %all-reduce.10 = (f32[128]{0:T(128)S(1)}, f32[128]{0:T(128)S(1)}) all-reduce(f32[128]{0:T(128)S(1)} %get-tuple-element.9, f32[128]{0:T(128)S(1)} %get-tuple-element.8), channel_id=1, replica_groups=mesh['dp'=64,'space'=8] {'space'}, use_global_device_ids=true, to_apply=%region_7.8 | all-reduce | flops 256 | bytes 2048 | tf_op jit(solution)/shard_map/psum | solution.py:73
  177.5 1.7 fusion.24
  179.2 16.0 %all-reduce.9 = (f32[128]{0:T(128)}, f32[128]{0:T(128)}) all-reduce(f32[128]{0:T(128)S(1)} %get-tuple-element.7, f32[128]{0:T(128)S(1)} %get-tuple-element.6), channel_id=1, replica_groups=mesh['dp'=64,'space'=8] {'space'}, use_global_device_ids=true, to_apply=%region_11.12 | all-reduce | flops 256 | bytes 2048 | tf_op jit(solution)/shard_map/psum | solution.py:81
  195.9 1.0 multiply_convert_fusion.1
  196.9 2.6 collective-permute-start.4
  199.5 1.5 collective-permute-start.5
  201.0 1.6 convolution_convert_fusion
  202.6 2.6 collective-permute-done.5
  207.5 16.7 %all-reduce.8 = (f32[128]{0:T(128)S(1)}, f32[128]{0:T(128)S(1)}) all-reduce(f32[128]{0:T(128)S(1)} %get-tuple-element.5, f32[128]{0:T(128)S(1)} %get-tuple-element.4), channel_id=1, replica_groups=mesh['dp'=64,'space'=8] {'space'}, use_global_device_ids=true, to_apply=%region_15.16 | all-reduce | flops 256 | bytes 2048 | tf_op jit(solution)/shard_map/psum | solution.py:81
  224.3 1.6 collective-permute-start.6
  225.9 1.3 collective-permute-start.7
  227.2 1.6 convolution_convert_fusion.1
  228.8 3.0 collective-permute-done.7
  232.0 0.8 fusion.29
  233.5 83.9 %all-reduce.16.cloned.1.call-done = (bf16[3456,128]{1,0:T(8,128)(2,1)}, bf16[3456,128]{1,0:T(8,128)(2,1)}) async-done(((bf16[3456,128]{1,0:T(8,128)(2,1)}, bf16[3456,128]{1,0:T(8,128)(2,1)}), (bf16[3456,128]{1,0:T(8,128)(2,1)}, bf16[3456,128]{1,0:T(8,128)(2,1)})) %all-reduce.16.cloned.1.call-update) | async-done | bytes 1769488 | tf_op jit(solution)/shard_map/psum | solution.py:98
  317.4 1.4 convert_element_type.50
  319.0 127.5 %fusion.27 = (f32[64,128]{1,0:T(8,128)}, f32[64,128]{1,0:T(8,128)}) fusion(f32[3456,128]{1,0:T(8,128)S(1)} %convert_element_type.50, f32[3456,128]{1,0:T(8,128)S(1)} %convert_element_type.52), kind=kCustom, calls=%all-reduce-scatter.2 | all-reduce-scatter fusion | flops 1048577 | bytes 3606528
  446.4 0.8 slice.606
  447.3 2.2 collective-permute-start.16
  449.5 6.2 %collective-permute-start.15 = (f32[64,128]{1,0:T(8,128)}, f32[64,128]{1,0:T(8,128)S(1)}, u32[]{:S(2)}, u32[]{:S(2)}) collective-permute-start(f32[64,128]{1,0:T(8,128)} %get-tuple-element.24), channel_id=1, source_target_pairs={{0,64},{8,72},{16,80},{24,88},{32,96},{40,104},{48,112},{56,120},{... | collective-permute-start | bytes 98312
  455.7 23.8 %collective-permute-start.14 = (f32[64,128]{1,0:T(8,128)}, f32[64,128]{1,0:T(8,128)S(1)}, u32[]{:S(2)}, u32[]{:S(2)}) collective-permute-start(f32[64,128]{1,0:T(8,128)} %get-tuple-element.24), channel_id=1, source_target_pairs={{0,56},{8,64},{16,72},{24,80},{32,88},{40,96},{48,104},{56,112},{6... | collective-permute-start | bytes 98312
  479.5 1.9 collective-permute-start.13
  481.4 1.3 collective-permute-start.17
  482.7 1.5 constant_dynamic-update-slice_fusion.82
  484.3 3.4 collective-permute-start.12
  487.7 8.2 %collective-permute-start.11 = (f32[64,128]{1,0:T(8,128)}, f32[64,128]{1,0:T(8,128)S(1)}, u32[]{:S(2)}, u32[]{:S(2)}) collective-permute-start(f32[64,128]{1,0:T(8,128)} %get-tuple-element.24), channel_id=1, source_target_pairs={{0,32},{8,40},{16,48},{24,56},{32,64},{40,72},{48,80},{56,88},{64,... | collective-permute-start | bytes 98312
  495.9 1.9 collective-permute-start.10
  497.8 1.9 collective-permute-start.9
  499.7 3.5 collective-permute-start.8
  503.2 1.5 constant_dynamic-update-slice_fusion.81
  504.7 0.8 slice.607
  505.4 2.3 collective-permute-start.26
  507.8 1.9 collective-permute-start.25
  509.7 2.7 collective-permute-start.24
  512.4 2.7 collective-permute-start.23
  515.1 1.6 collective-permute-start.27
  516.7 3.0 fusion.2
  519.8 1.6 concatenate.380
  521.4 2.7 collective-permute-start.22
  524.1 4.6 collective-permute-start.21
  528.7 1.9 collective-permute-start.20
  530.7 1.9 collective-permute-start.19
  532.6 3.8 collective-permute-start.18
  537.1 1.5 collective-permute-done.19
  538.6 2.9 collective-permute-done.18
  541.5 1.6 concatenate.381
  (206 shorter events, 9.2 us)
Async XLA Ops:
  7.2 58.2 %copy-start.15 = (bf16[54,128]{1,0:T(8,128)(2,1)S(1)}, bf16[54,128]{1,0:T(8,128)(2,1)}, u32[]{:S(2)}) copy-start(bf16[54,128]{1,0:T(8,128)(2,1)} %param.7) | copy-start | bytes 41476
  7.2 310.2 %all-reduce.16.cloned.1.call-start = ((), (), s32[]{:S(2)}) async-start(), calls=%async_computation | async-start | bytes 3538944 | tf_op jit(solution)/shard_map/psum | solution.py:98
  8.0 111.1 %collective-permute-start = (bf16[1,8,8,128]{3,2,1,0:T(8,128)(2,1)S(1)}, bf16[1,8,8,128]{3,2,1,0:T(8,128)(2,1)S(1)}, u32[]{:S(2)}, u32[]{:S(2)}) collective-permute-start(bf16[1,8,8,128]{3,2,1,0:T(8,128)(2,1)S(1)} %get-tuple-element.138), channel_id=1, source_target_pairs={{0,1},{1,2},{2,3},{3,4},{4,5},{5,6},{6,7},{8,9},{9,10},{10,11},{11... | collective-permute-start | bytes 49160 | tf_op jit(solution)/shard_map/ppermute | solution.py:19
  12.2 106.8 %collective-permute-start.1 = (bf16[1,8,8,128]{3,2,1,0:T(8,128)(2,1)S(1)}, bf16[1,8,8,128]{3,2,1,0:T(8,128)(2,1)S(1)}, u32[]{:S(2)}, u32[]{:S(2)}) collective-permute-start(bf16[1,8,8,128]{3,2,1,0:T(8,128)(2,1)S(1)} %get-tuple-element.139), channel_id=1, source_target_pairs={{1,0},{2,1},{3,2},{4,3},{5,4},{6,5},{7,6},{9,8},{10,9},{11,10},{12... | collective-permute-start | bytes 49160 | tf_op jit(solution)/shard_map/ppermute | solution.py:21
  116.8 2.3 copy-start.7
  119.5 1.2 copy-start.1
  121.3 29.5 %copy-start.3 = (f32[256,128]{1,0:T(8,128)}, f32[256,128]{1,0:T(8,128)S(1)}, u32[]{:S(2)}) copy-start(f32[256,128]{1,0:T(8,128)S(1)} %get-tuple-element.144) | copy-start | bytes 393220
  144.8 1.4 copy-start.16
  144.8 1.4 copy-start.19
  144.8 11.9 %copy-start.10 = (bf16[256,128]{1,0:T(8,128)(2,1)}, bf16[256,128]{1,0:T(8,128)(2,1)S(1)}, u32[]{:S(2)}) copy-start(bf16[256,128]{1,0:T(8,128)(2,1)S(1)} %multiply_convert_fusion.3) | copy-start | bytes 196612
  144.9 11.8 %collective-permute-start.2 = (bf16[1,8,8,128]{3,2,1,0:T(8,128)(2,1)S(1)}, bf16[1,8,8,128]{3,2,1,0:T(8,128)(2,1)S(1)}, u32[]{:S(2)}, u32[]{:S(2)}) collective-permute-start(bf16[1,8,8,128]{3,2,1,0:T(8,128)(2,1)S(1)} %get-tuple-element.134), channel_id=1, source_target_pairs={{0,1},{1,2},{2,3},{3,4},{4,5},{5,6},{6,7},{8,9},{9,10},{10,11},{11... | collective-permute-start | bytes 49160 | tf_op jit(solution)/shard_map/ppermute | solution.py:19
  146.2 10.5 %collective-permute-start.3 = (bf16[1,8,8,128]{3,2,1,0:T(8,128)(2,1)S(1)}, bf16[1,8,8,128]{3,2,1,0:T(8,128)(2,1)S(1)}, u32[]{:S(2)}, u32[]{:S(2)}) collective-permute-start(bf16[1,8,8,128]{3,2,1,0:T(8,128)(2,1)S(1)} %get-tuple-element.135), channel_id=1, source_target_pairs={{1,0},{2,1},{3,2},{4,3},{5,4},{6,5},{7,6},{9,8},{10,9},{11,10},{12... | collective-permute-start | bytes 49160 | tf_op jit(solution)/shard_map/ppermute | solution.py:21
  150.8 2.3 copy-start.2
  156.7 0.6 copy-start.14
  156.8 0.8 copy-start.11
  156.9 1.7 copy-start.4
  156.9 1.7 copy-start.17
  156.9 1.7 copy-start.20
  157.4 1.7 copy-start
  196.9 5.7 %collective-permute-start.4 = (bf16[1,8,8,128]{3,2,1,0:T(8,128)(2,1)S(1)}, bf16[1,8,8,128]{3,2,1,0:T(8,128)(2,1)S(1)}, u32[]{:S(2)}, u32[]{:S(2)}) collective-permute-start(bf16[1,8,8,128]{3,2,1,0:T(8,128)(2,1)S(1)} %get-tuple-element.130), channel_id=1, source_target_pairs={{0,1},{1,2},{2,3},{3,4},{4,5},{5,6},{6,7},{8,9},{9,10},{10,11},{11... | collective-permute-start | bytes 49160 | tf_op jit(solution)/shard_map/ppermute | solution.py:19
  199.5 5.7 %collective-permute-start.5 = (bf16[1,8,8,128]{3,2,1,0:T(8,128)(2,1)S(1)}, bf16[1,8,8,128]{3,2,1,0:T(8,128)(2,1)S(1)}, u32[]{:S(2)}, u32[]{:S(2)}) collective-permute-start(bf16[1,8,8,128]{3,2,1,0:T(8,128)(2,1)S(1)} %get-tuple-element.131), channel_id=1, source_target_pairs={{1,0},{2,1},{3,2},{4,3},{5,4},{6,5},{7,6},{9,8},{10,9},{11,10},{12... | collective-permute-start | bytes 49160 | tf_op jit(solution)/shard_map/ppermute | solution.py:21
  205.6 0.9 copy-start.5
  205.6 1.2 copy-start.8
  205.6 1.2 copy-start.18
  205.6 1.2 copy-start.21
  224.3 4.6 collective-permute-start.6
  225.9 5.9 %collective-permute-start.7 = (bf16[1,8,8,128]{3,2,1,0:T(8,128)(2,1)S(1)}, bf16[1,8,8,128]{3,2,1,0:T(8,128)(2,1)S(1)}, u32[]{:S(2)}, u32[]{:S(2)}) collective-permute-start(bf16[1,8,8,128]{3,2,1,0:T(8,128)(2,1)S(1)} %get-tuple-element.127), channel_id=1, source_target_pairs={{1,0},{2,1},{3,2},{4,3},{5,4},{6,5},{7,6},{9,8},{10,9},{11,10},{12... | collective-permute-start | bytes 49160 | tf_op jit(solution)/shard_map/ppermute | solution.py:21
  233.4 84.0 %copy-start.6 = (bf16[256,3456]{1,0:T(8,128)(2,1)}, bf16[256,3456]{1,0:T(8,128)(2,1)S(1)}, u32[]{:S(2)}) copy-start(bf16[256,3456]{1,0:T(8,128)(2,1)S(1)} %constant_dynamic-update-slice_fusion.83) | copy-start | bytes 5308420
  317.4 1.4 copy-start.9
  446.4 73.3 %copy-start.13 = (f32[64,128]{1,0:T(8,128)S(1)}, f32[64,128]{1,0:T(8,128)}, u32[]{:S(2)}) copy-start(f32[64,128]{1,0:T(8,128)} %get-tuple-element.24) | copy-start | bytes 98308
  447.3 40.4 %collective-permute-start.16 = (f32[64,128]{1,0:T(8,128)}, f32[64,128]{1,0:T(8,128)S(1)}, u32[]{:S(2)}, u32[]{:S(2)}) collective-permute-start(f32[64,128]{1,0:T(8,128)} %get-tuple-element.24), channel_id=1, source_target_pairs={{0,72},{8,80},{16,88},{24,96},{32,104},{40,112},{48,120},{56,128},... | collective-permute-start | bytes 98312
  449.5 46.4 %collective-permute-start.15 = (f32[64,128]{1,0:T(8,128)}, f32[64,128]{1,0:T(8,128)S(1)}, u32[]{:S(2)}, u32[]{:S(2)}) collective-permute-start(f32[64,128]{1,0:T(8,128)} %get-tuple-element.24), channel_id=1, source_target_pairs={{0,64},{8,72},{16,80},{24,88},{32,96},{40,104},{48,112},{56,120},{... | collective-permute-start | bytes 98312
  455.7 42.1 %collective-permute-start.14 = (f32[64,128]{1,0:T(8,128)}, f32[64,128]{1,0:T(8,128)S(1)}, u32[]{:S(2)}, u32[]{:S(2)}) collective-permute-start(f32[64,128]{1,0:T(8,128)} %get-tuple-element.24), channel_id=1, source_target_pairs={{0,56},{8,64},{16,72},{24,80},{32,88},{40,96},{48,104},{56,112},{6... | collective-permute-start | bytes 98312
  479.5 20.2 %collective-permute-start.13 = (f32[64,128]{1,0:T(8,128)}, f32[64,128]{1,0:T(8,128)S(1)}, u32[]{:S(2)}, u32[]{:S(2)}) collective-permute-start(f32[64,128]{1,0:T(8,128)} %get-tuple-element.24), channel_id=1, source_target_pairs={{0,48},{8,56},{16,64},{24,72},{32,80},{40,88},{48,96},{56,104},{64... | collective-permute-start | bytes 98312
  481.4 2.8 collective-permute-start.17
  484.3 21.2 %collective-permute-start.12 = (f32[64,128]{1,0:T(8,128)}, f32[64,128]{1,0:T(8,128)S(1)}, u32[]{:S(2)}, u32[]{:S(2)}) collective-permute-start(f32[64,128]{1,0:T(8,128)} %get-tuple-element.24), channel_id=1, source_target_pairs={{0,40},{8,48},{16,56},{24,64},{32,72},{40,80},{48,88},{56,96},{64,... | collective-permute-start | bytes 98312
  487.7 20.1 %collective-permute-start.11 = (f32[64,128]{1,0:T(8,128)}, f32[64,128]{1,0:T(8,128)S(1)}, u32[]{:S(2)}, u32[]{:S(2)}) collective-permute-start(f32[64,128]{1,0:T(8,128)} %get-tuple-element.24), channel_id=1, source_target_pairs={{0,32},{8,40},{16,48},{24,56},{32,64},{40,72},{48,80},{56,88},{64,... | collective-permute-start | bytes 98312
  495.9 13.9 %collective-permute-start.10 = (f32[64,128]{1,0:T(8,128)}, f32[64,128]{1,0:T(8,128)S(1)}, u32[]{:S(2)}, u32[]{:S(2)}) collective-permute-start(f32[64,128]{1,0:T(8,128)} %get-tuple-element.24), channel_id=1, source_target_pairs={{0,24},{8,32},{16,40},{24,48},{32,56},{40,64},{48,72},{56,80},{64,... | collective-permute-start | bytes 98312
  497.8 14.6 %collective-permute-start.9 = (f32[64,128]{1,0:T(8,128)}, f32[64,128]{1,0:T(8,128)S(1)}, u32[]{:S(2)}, u32[]{:S(2)}) collective-permute-start(f32[64,128]{1,0:T(8,128)} %get-tuple-element.24), channel_id=1, source_target_pairs={{0,16},{8,24},{16,32},{24,40},{32,48},{40,56},{48,64},{56,72},{64,... | collective-permute-start | bytes 98312
  499.7 15.4 %collective-permute-start.8 = (f32[64,128]{1,0:T(8,128)}, f32[64,128]{1,0:T(8,128)S(1)}, u32[]{:S(2)}, u32[]{:S(2)}) collective-permute-start(f32[64,128]{1,0:T(8,128)} %get-tuple-element.24), channel_id=1, source_target_pairs={{0,8},{8,16},{16,24},{24,32},{32,40},{40,48},{48,56},{56,64},{64,7... | collective-permute-start | bytes 98312
  505.4 18.7 %collective-permute-start.26 = (f32[64,128]{1,0:T(8,128)}, f32[64,128]{1,0:T(8,128)S(1)}, u32[]{:S(2)}, u32[]{:S(2)}) collective-permute-start(f32[64,128]{1,0:T(8,128)} %get-tuple-element.25), channel_id=1, source_target_pairs={{0,72},{8,80},{16,88},{24,96},{32,104},{40,112},{48,120},{56,128},... | collective-permute-start | bytes 98312
  507.8 20.9 %collective-permute-start.25 = (f32[64,128]{1,0:T(8,128)}, f32[64,128]{1,0:T(8,128)S(1)}, u32[]{:S(2)}, u32[]{:S(2)}) collective-permute-start(f32[64,128]{1,0:T(8,128)} %get-tuple-element.25), channel_id=1, source_target_pairs={{0,64},{8,72},{16,80},{24,88},{32,96},{40,104},{48,112},{56,120},{... | collective-permute-start | bytes 98312
  509.7 20.9 %collective-permute-start.24 = (f32[64,128]{1,0:T(8,128)}, f32[64,128]{1,0:T(8,128)S(1)}, u32[]{:S(2)}, u32[]{:S(2)}) collective-permute-start(f32[64,128]{1,0:T(8,128)} %get-tuple-element.25), channel_id=1, source_target_pairs={{0,56},{8,64},{16,72},{24,80},{32,88},{40,96},{48,104},{56,112},{6... | collective-permute-start | bytes 98312
  512.4 20.2 %collective-permute-start.23 = (f32[64,128]{1,0:T(8,128)}, f32[64,128]{1,0:T(8,128)S(1)}, u32[]{:S(2)}, u32[]{:S(2)}) collective-permute-start(f32[64,128]{1,0:T(8,128)} %get-tuple-element.25), channel_id=1, source_target_pairs={{0,48},{8,56},{16,64},{24,72},{32,80},{40,88},{48,96},{56,104},{64... | collective-permute-start | bytes 98312
  515.1 6.3 %collective-permute-start.27 = (f32[54,128]{1,0:T(8,128)S(1)}, f32[54,128]{1,0:T(8,128)S(1)}, u32[]{:S(2)}, u32[]{:S(2)}) collective-permute-start(f32[54,128]{1,0:T(8,128)S(1)} %slice.607), channel_id=1, source_target_pairs={{0,80},{8,88},{16,96},{24,104},{32,112},{40,120},{48,128},{56,136}... | collective-permute-start | bytes 82952
  516.7 4.7 copy-start.12
  521.4 15.7 %collective-permute-start.22 = (f32[64,128]{1,0:T(8,128)S(1)}, f32[64,128]{1,0:T(8,128)S(1)}, u32[]{:S(2)}, u32[]{:S(2)}) collective-permute-start(f32[64,128]{1,0:T(8,128)S(1)} %copy-done.12), channel_id=1, source_target_pairs={{0,40},{8,48},{16,56},{24,64},{32,72},{40,80},{48,88},{56,96},{64,... | collective-permute-start | bytes 98312
  524.1 13.0 %collective-permute-start.21 = (f32[64,128]{1,0:T(8,128)S(1)}, f32[64,128]{1,0:T(8,128)S(1)}, u32[]{:S(2)}, u32[]{:S(2)}) collective-permute-start(f32[64,128]{1,0:T(8,128)S(1)} %copy-done.12), channel_id=1, source_target_pairs={{0,32},{8,40},{16,48},{24,56},{32,64},{40,72},{48,80},{56,88},{64,... | collective-permute-start | bytes 98312
  528.7 8.4 %collective-permute-start.20 = (f32[64,128]{1,0:T(8,128)S(1)}, f32[64,128]{1,0:T(8,128)S(1)}, u32[]{:S(2)}, u32[]{:S(2)}) collective-permute-start(f32[64,128]{1,0:T(8,128)S(1)} %copy-done.12), channel_id=1, source_target_pairs={{0,24},{8,32},{16,40},{24,48},{32,56},{40,64},{48,72},{56,80},{64,... | collective-permute-start | bytes 98312
  530.7 7.9 %collective-permute-start.19 = (f32[64,128]{1,0:T(8,128)S(1)}, f32[64,128]{1,0:T(8,128)S(1)}, u32[]{:S(2)}, u32[]{:S(2)}) collective-permute-start(f32[64,128]{1,0:T(8,128)S(1)} %copy-done.12), channel_id=1, source_target_pairs={{0,16},{8,24},{16,32},{24,40},{32,48},{40,56},{48,64},{56,72},{64,... | collective-permute-start | bytes 98312
  532.6 8.8 %collective-permute-start.18 = (f32[64,128]{1,0:T(8,128)S(1)}, f32[64,128]{1,0:T(8,128)S(1)}, u32[]{:S(2)}, u32[]{:S(2)}) collective-permute-start(f32[64,128]{1,0:T(8,128)S(1)} %copy-done.12), channel_id=1, source_target_pairs={{0,8},{8,16},{16,24},{24,32},{32,40},{40,48},{48,56},{56,64},{64,7... | collective-permute-start | bytes 98312
Sparse Core Ops, SparseCore 0:
  229.0 88.3 all-reduce.15
where the time goes:
time: 552 us; the launch traced here: 551 us
  blocking collectives  301 us (55%)
  starting transfers between devices  95.6 us (17%)
  waiting for transfers between devices  94 us (17%)
  local copies, waits for them, and re-layouts  28.1 us (5%)
  between operations  16.1 us (3%)
  matrix products  8.77 us (2%)
  other arithmetic  7.44 us (1%)
    unnamed x1, blocking collectives  127 us
    all_gather x2, blocking collectives, apply_weight(): whole = lax.all_gather(shard, 'dp', axis=0, tiled=True)  99.9 us
    psum x1, waiting for transfers between devices, reduce_grad(): lax.psum(local.astype(jnp.bfloat16), 'space').astype(jnp.float32)  83.9 us
    unnamed x20, starting transfers between devices  80.4 us
    psum x2, blocking collectives, normalize(): lax.psum((jnp.sum(values, axis=0), jnp.sum(values * values, axis=0)), 'sp...  40.6 us
    psum x2, blocking collectives, norm_back(): lax.psum((jnp.sum(grad, axis=0), jnp.sum(grad * normed, axis=0)), 'space')  32.7 us
    unnamed x154, local copies, waits for them, and re-layouts  13.5 us
  transfers between devices with their start and end apart: 29, of which 5 were waited for; matrix products, arithmetic and copies ran while one was open for 5% of the time, Pallas kernels for 0%

commit v1 on v0

v1 whole, which is shorter than its diff:
```python
import functools
import math

import jax
import jax.numpy as jnp
from jax import lax
from jax.experimental import pallas as pl
from jax.experimental.pallas import tpu as pltpu
from jax.sharding import Mesh, PartitionSpec as P


EPSILON = 1e-05
C = 128
H = 8
W = 8
PLANE = H * W
TAPS = 27
NINE = 9 * C
ROWS = TAPS * C
BLOCK = 256
MATRIX = 512
SPLIT = 8

bf16 = jnp.bfloat16
f32 = jnp.float32


def phi_parts(u):
    cdf = 0.5 * (1.0 + lax.erf(u * 0.7071067811865476))
    return cdf


def slope_of(u, cdf):
    return cdf + u * jnp.exp(-0.5 * u * u) * 0.3989422804014327


def shifts_of(x):
    w_at = lax.broadcasted_iota(jnp.int32, x.shape, 2)
    left = jnp.where(w_at >= 1, pltpu.roll(x, 1, axis=2), 0.0)
    right = jnp.where(w_at <= W - 2, pltpu.roll(x, W - 1, axis=2), 0.0)
    zero = jnp.zeros_like(x[:, :1])
    out = []
    for b in range(3):
        for y in (left, x, right):
            if b == 0:
                y = jnp.concatenate([zero, y[:, : H - 1]], axis=1)
            elif b == 2:
                y = jnp.concatenate([y[:, 1:], zero], axis=1)
            out.append(y)
    return out


def build_nine(load, nine, planes, first=0):
    step = 2

    def one(i, _):
        x = load(i * step, step).astype(f32).reshape(step, H, W, C)
        row = pl.multiple_of((i * step + 1 + first) * PLANE, PLANE)
        for k, y in enumerate(shifts_of(x)):
            nine[pl.ds(row, step * PLANE), k * C : (k + 1) * C] = y.reshape(
                step * PLANE, C
            ).astype(bf16)
        return 0

    lax.fori_loop(0, planes // step, one, 0)


def clear_ends(nine, planes):
    zero = jnp.zeros((PLANE, NINE), bf16)
    nine[0:PLANE, :] = zero
    nine[(planes + 1) * PLANE : (planes + 2) * PLANE, :] = zero


def plane_loader(ref):
    return lambda d, n: ref[pl.ds(pl.multiple_of(d * PLANE, PLANE), n * PLANE), :]


def conv_rows(nine, weight, row, rows):
    acc = None
    for a in range(3):
        part = jnp.dot(
            nine[pl.ds(pl.multiple_of(row + a * PLANE, PLANE), rows), :],
            weight[a * NINE : (a + 1) * NINE, :],
            preferred_element_type=f32,
        )
        acc = part if acc is None else acc + part
    return acc


def reverse_into(weight, out):
    for k in range(TAPS):
        block = weight[(TAPS - 1 - k) * C : (TAPS - k) * C, :]
        out[k * C : (k + 1) * C, :] = block.astype(f32).T.astype(bf16)


def assemble(core, mine, theirs, flat, weight):
    chips = mine.shape[0]
    part = ROWS // (2 * chips)
    mine_first = core == 0
    for y in range(chips):
        one = mine[y].astype(f32)
        two = theirs[y].astype(f32)
        even = jnp.where(mine_first, one, two)[:part]
        odd = jnp.where(mine_first, two, one)[:part]
        flat[2 * y * part : (2 * y + 1) * part, :] = even
        flat[(2 * y + 1) * part : (2 * y + 2) * part, :] = odd
    for k in range(TAPS):
        weight[k * C : (k + 1) * C, :] = flat[k * C : (k + 1) * C, :].astype(bf16)


def row_sum(x):
    return jnp.sum(x, axis=0, keepdims=True)


def grad_into(nine, delta, cells, three, turned, flat, out, place):
    rows = cells + 2 * PLANE
    for a in range(3):
        cols = slice(a * C, (a + 1) * C)
        if a:
            three[0 : a * PLANE, cols] = jnp.zeros((a * PLANE, C), bf16)
        three[a * PLANE : a * PLANE + cells, cols] = delta[...]
        if a < 2:
            three[a * PLANE + cells : rows, cols] = jnp.zeros(((2 - a) * PLANE, C), bf16)

    def turn(i, _):
        at = pl.multiple_of(i * C, C)
        for a in range(3):
            block = three[pl.ds(at, C), a * C : (a + 1) * C].astype(f32)
            turned[a * C : (a + 1) * C, pl.ds(at, C)] = block.T.astype(bf16)
        return 0

    lax.fori_loop(0, rows // C, turn, 0)

    def product(n, _):
        at = pl.multiple_of(n * 3 * C, 3 * C)
        total = jnp.dot(
            turned[...], nine[:, pl.ds(at, 3 * C)], preferred_element_type=f32
        )
        for a in range(3):
            for i in range(3):
                block = total[a * C : (a + 1) * C, i * C : (i + 1) * C].T
                flat[pl.ds(pl.multiple_of(a * NINE + at + i * C, C), C), :] = block
        return 0

    lax.fori_loop(0, 3, product, 0)
    shares, tall, _ = out.shape
    part = ROWS // shares
    base = place[0] * (-(-part // SPLIT))
    for j in range(shares):
        out[j] = flat[pl.ds(j * part + base, tall), :].astype(bf16)


def first_kernel(
    place, image, mine, theirs,
    normed, hidden, inverse_out, weight,
    nine, conv, flat,
):
    cells = image.shape[0]
    planes = cells // PLANE
    assemble(place[1], mine, theirs, flat, weight)
    clear_ends(nine, planes)
    build_nine(plane_loader(image), nine, planes)

    def one(i, sums):
        row = pl.multiple_of(i * MATRIX, MATRIX)
        acc = conv_rows(nine, weight, row, MATRIX)
        conv[pl.ds(row, MATRIX), :] = acc
        return (sums[0] + row_sum(acc), sums[1] + row_sum(acc * acc))

    zero = jnp.zeros((1, C), f32)
    total, square = lax.fori_loop(0, cells // MATRIX, one, (zero, zero))
    average = total / cells
    inverse = lax.rsqrt(square / cells - average * average + EPSILON)
    inverse_out[...] = jnp.broadcast_to(inverse, inverse_out.shape)

    def two(i, _):
        at = pl.ds(pl.multiple_of(i * BLOCK, BLOCK), BLOCK)
        u = (conv[at, :] - average) * inverse
        normed[at, :] = u
        hidden[at, :] = (u * phi_parts(u)).astype(bf16)
        return 0

    lax.fori_loop(0, cells // BLOCK, two, 0)


def second_kernel(
    place, hidden, mine, theirs, image, cotangent,
    output, outer_slab, delta, grads, weight,
    nine, conv, outer, three, turned, flat,
):
    cells = hidden.shape[0]
    planes = cells // PLANE
    assemble(place[1], mine, theirs, flat, weight)
    clear_ends(nine, planes)
    build_nine(plane_loader(hidden), nine, planes)

    def one(i, sums):
        row = pl.multiple_of(i * MATRIX, MATRIX)
        acc = conv_rows(nine, weight, row, MATRIX)
        conv[pl.ds(row, MATRIX), :] = acc
        return (sums[0] + row_sum(acc), sums[1] + row_sum(acc * acc))

    zero = jnp.zeros((1, C), f32)
    total, square = lax.fori_loop(0, cells // MATRIX, one, (zero, zero))
    average = total / cells
    inverse = lax.rsqrt(square / cells - average * average + EPSILON)
    slab = output.shape[0]

    def two(i, sums):
        at = pl.ds(pl.multiple_of(i * slab, slab), slab)
        n = (conv[at, :] - average) * inverse
        conv[at, :] = n
        u = image[at, :].astype(f32) + n
        cdf = phi_parts(u)
        grad = cotangent[at, :].astype(f32) * slope_of(u, cdf)
        outer[at, :] = grad

        @pl.when(i == place[0])
        def _():
            output[...] = (u * cdf).astype(bf16)
            outer_slab[...] = grad

        return (sums[0] + row_sum(grad), sums[1] + row_sum(grad * n))

    plain, paired = lax.fori_loop(0, cells // slab, two, (zero, zero))
    plain = plain / cells
    paired = paired / cells

    def three_(i, _):
        at = pl.ds(pl.multiple_of(i * BLOCK, BLOCK), BLOCK)
        delta[at, :] = (inverse * (outer[at, :] - plain - conv[at, :] * paired)).astype(bf16)
        return 0

    lax.fori_loop(0, cells // BLOCK, three_, 0)
    grad_into(nine, delta, cells, three, turned, flat, grads, place)


def third_kernel(
    place, second_delta, weight, normed, inverse, image,
    delta, grads,
    nine, conv, turned_weight, three, turned, flat,
):
    cells = image.shape[0]
    planes = cells // PLANE
    clear_ends(nine, planes)
    reverse_into(weight, turned_weight)
    build_nine(plane_loader(second_delta), nine, planes)

    def one(i, sums):
        row = pl.multiple_of(i * MATRIX, MATRIX)
        at = pl.ds(row, MATRIX)
        acc = conv_rows(nine, turned_weight, row, MATRIX)
        u = normed[at, :]
        grad = acc * slope_of(u, phi_parts(u))
        conv[at, :] = grad
        return (sums[0] + row_sum(grad), sums[1] + row_sum(grad * u))

    zero = jnp.zeros((1, C), f32)
    plain, paired = lax.fori_loop(0, cells // MATRIX, one, (zero, zero))
    plain = plain / cells
    paired = paired / cells
    scale = inverse[0:1, :]

    def two(i, _):
        at = pl.ds(pl.multiple_of(i * BLOCK, BLOCK), BLOCK)
        delta[at, :] = (scale * (conv[at, :] - plain - normed[at, :] * paired)).astype(bf16)
        return 0

    lax.fori_loop(0, cells // BLOCK, two, 0)
    build_nine(plane_loader(image), nine, planes)
    grad_into(nine, delta, cells, three, turned, flat, grads, place)


def fourth_kernel(place, delta, weight, outer_slab, grad, nine, turned_weight):
    slab = grad.shape[0]
    planes = slab // PLANE
    last = delta.shape[0] // PLANE
    reverse_into(weight, turned_weight)
    base = place[0] * planes
    for p in range(planes + 2):
        d = base + (p - 1)
        inside = jnp.logical_and(d >= 0, d < last)
        at = pl.multiple_of(jnp.clip(d, 0, last - 1) * PLANE, PLANE)
        x = delta[pl.ds(at, PLANE), :].astype(f32)
        x = jnp.where(inside, x, 0.0).reshape(1, H, W, C)
        for k, y in enumerate(shifts_of(x)):
            nine[p * PLANE : (p + 1) * PLANE, k * C : (k + 1) * C] = y.reshape(
                PLANE, C
            ).astype(bf16)
    grad[...] = (outer_slab[...] + conv_rows(nine, turned_weight, 0, slab)).astype(bf16)


SMEM = pl.BlockSpec(memory_space=pltpu.SMEM)
VMEM = pl.BlockSpec(memory_space=pltpu.VMEM)


def call(kernel, outs, scratch, *args, mib=4):
    specs = []
    for a in args:
        if isinstance(a, tuple):
            whole, half = a
            shape = (whole.shape[0], whole.shape[1] // 2, C)
            specs.append(pl.BlockSpec(shape, functools.partial(lambda h, i: (0, h, 0), half)))
        else:
            specs.append(SMEM if a.dtype == jnp.int32 else VMEM)
    args = [a[0] if isinstance(a, tuple) else a for a in args]
    return pl.pallas_call(
        kernel,
        grid=(1,),
        out_shape=tuple(jax.ShapeDtypeStruct(s, d) for s, d in outs),
        in_specs=specs,
        out_specs=tuple(VMEM for _ in outs),
        scratch_shapes=[pltpu.VMEM(s, d) for s, d in scratch],
        compiler_params=pltpu.CompilerParams(vmem_limit_bytes=mib * 1024 * 1024),
    )(*args)


def first_call(place, image, mine, theirs):
    cells = image.shape[0]
    return call(
        first_kernel,
        [((cells, C), f32), ((cells, C), bf16), ((8, C), f32), ((ROWS, C), bf16)],
        [((cells + 2 * PLANE, NINE), bf16), ((cells, C), f32), ((ROWS + 8, C), f32)],
        place, image, (mine, 0), (theirs, 0), mib=16,
    )


def grad_scratch(cells):
    return [
        ((cells + 2 * PLANE, 3 * C), bf16),
        ((3 * C, cells + 2 * PLANE), bf16),
        ((ROWS + 8, C), f32),
    ]


def second_call(place, hidden, mine, theirs, image, cotangent, slab, chunks):
    cells = hidden.shape[0]
    return call(
        second_kernel,
        [
            ((slab, C), bf16), ((slab, C), f32), ((cells, C), bf16), (chunks, bf16),
            ((ROWS, C), bf16),
        ],
        [((cells + 2 * PLANE, NINE), bf16), ((cells, C), f32), ((cells, C), f32)]
        + grad_scratch(cells),
        place, hidden, (mine, 1), (theirs, 1), image, cotangent, mib=24,
    )


def third_call(place, second_delta, weight, normed, inverse, image, chunks):
    cells = image.shape[0]
    return call(
        third_kernel,
        [((cells, C), bf16), (chunks, bf16)],
        [((cells + 2 * PLANE, NINE), bf16), ((cells, C), f32), ((ROWS, C), bf16)]
        + grad_scratch(cells),
        place, second_delta, weight, normed, inverse, image, mib=24,
    )


def fourth_call(place, delta, weight, outer_slab):
    slab = outer_slab.shape[0]
    return call(
        fourth_kernel,
        [((slab, C), bf16)],
        [((slab + 2 * PLANE, NINE), bf16), ((ROWS, C), bf16)],
        place, delta, weight, outer_slab, mib=8,
    )[0]


def total_kernel(factor, first, second, both):
    tall = first.shape[1]
    for n, x in enumerate((first, second)):
        both[n * tall : (n + 1) * tall, :] = jnp.sum(x[...].astype(f32), axis=0) * factor


def total_call(first, second, factor):
    tall = first.shape[1]
    return call(
        functools.partial(total_kernel, factor),
        [((2 * tall, C), f32)], [], first, second,
    )[0]


def join_kernel(pieces, first, second):
    split, both, _ = pieces.shape
    tall = both // 2
    part = first.shape[0]
    piece = -(-part // split)
    for n, out in enumerate((first, second)):
        for s in range(split):
            rows = min(piece, part - s * piece)
            out[s * piece : s * piece + rows, :] = pieces[s, n * tall : n * tall + rows, :]


def join_call(pieces, part):
    return call(join_kernel, [((part, C), f32), ((part, C), f32)], [], pieces)


def spread(x, axes, count):
    copies = jnp.broadcast_to(x[None], (count,) + x.shape)
    return lax.all_to_all(copies, axes, 0, 0, tiled=True)


def solution(mesh):
    dp, space = mesh.shape["dp"], mesh.shape["space"]
    across = 4
    fine = Mesh(
        mesh.devices.reshape(dp // (2 * across), across, 2, space),
        ("y", "x", "core", "space"),
    )
    chips = dp // 2
    swap = [(0, 1), (1, 0)]
    plane = ("y", "x", "core")

    def step(image, cotangent, first_weight, second_weight):
        slab = image.shape[1] * PLANE
        cells = slab * space
        part = first_weight.shape[0]
        padded = -(-part // 8) * 8
        piece = -(-part // space)
        chunks = (dp, -(-piece // 8) * 8, C)
        factor = 1.0 / math.sqrt(cells * dp)
        core = lax.axis_index("core")
        place = jnp.stack([lax.axis_index("space"), core]).astype(jnp.int32)

        tall = ((0, padded - part), (0, 0))
        shard = jnp.concatenate([jnp.pad(first_weight, tall), jnp.pad(second_weight, tall)])
        mine = spread(shard, ("y", "x"), chips)
        patch = lax.all_gather(image.reshape(slab, C), "space", axis=0, tiled=True)
        theirs = lax.ppermute(mine, "core", swap)
        outer = spread(cotangent.reshape(slab, C), "space", space).reshape(cells, C)
        normed, hidden, inverse, w1 = first_call(place, patch, mine, theirs)
        output, outer_slab, second_delta, grads2, w2 = second_call(
            place, hidden, mine, theirs, patch, outer, slab, chunks
        )
        parts2 = lax.all_to_all(grads2, plane, 0, 0, tiled=True)
        first_delta, grads1 = third_call(
            place, second_delta, w2, normed, inverse, patch, chunks
        )
        parts1 = lax.all_to_all(grads1, plane, 0, 0, tiled=True)
        image_grad = fourth_call(place, first_delta, w1, outer_slab)
        pieces = spread(total_call(parts1, parts2, factor), "space", space)
        first_grad, second_grad = join_call(pieces, part)
        return (
            output.reshape(image.shape),
            image_grad.reshape(image.shape),
            first_grad,
            second_grad,
        )

    dp_axes = ("y", "x", "core")
    field = P(dp_axes, "space", None, None, None)
    rows = P(dp_axes, None)
    return jax.shard_map(
        step,
        mesh=fine,
        in_specs=(field, field, rows, rows),
        out_specs=(field, field, rows, rows),
        check_vma=False,
    )
```

time: 552 us -> 166 us (0.30)
  the two profiles are of different devices: /device:TPU:8 before, /device:TPU:1 now
where the time goes in v1:
time: 166 us; the launch traced here: 165 us
  blocking collectives  101 us (61%)
  Pallas kernels  34 us (20%)
  starting transfers between devices  20 us (12%)
  waiting for transfers between devices  5.3 us (3%)
  local copies, waits for them, and re-layouts  3.54 us (2%)
    all_to_all x1, blocking collectives, spread(): return lax.all_to_all(copies, axes, 0, 0, tiled=True)  34 us
    pallas_call x6, Pallas kernels, call(): pl.pallas_call(kernel, grid=(1,), out_shape=tuple((jax.ShapeDtypeStruct(s...  34 us
    all_gather x1, blocking collectives, step(): patch = lax.all_gather(image.reshape(slab, C), 'space', axis=0, tiled=True)  29.1 us
    all_to_all x1, blocking collectives, step(): parts1 = lax.all_to_all(grads1, plane, 0, 0, tiled=True)  22.6 us
    all_to_all x2, starting transfers between devices, spread(): return lax.all_to_all(copies, axes, 0, 0, tiled=True)  15.2 us
    all_to_all x1, blocking collectives, step(): parts2 = lax.all_to_all(grads2, plane, 0, 0, tiled=True)  14.9 us
    all_to_all x2, waiting for transfers between devices, spread(): return lax.all_to_all(copies, axes, 0, 0, tiled=True)  5.3 us
    ppermute x1, starting transfers between devices, step(): theirs = lax.ppermute(mine, 'core', swap)  4.79 us
  transfers between devices with their start and end apart: 3, of which 1 were waited for; matrix products, arithmetic and copies ran while one was open for 1% of the time, Pallas kernels for 5%

profile of v1, /device:TPU:1, one launch (start us, length us, event | category | flops | bytes accessed | tf_op | source)
XLA Modules:
  0.0 165.1 jit_solution(3828740740661487045)
XLA Ops:
  0.6 0.7 fusion.2
  1.4 0.1 broadcast_in_dim.8
  1.5 0.0 copy-start.4
  1.5 34.0 %all_to_all.25.mine = bf16[32,112,128]{2,1,0:T(8,128)(2,1)S(1)} all-to-all(bf16[32,112,128]{2,1,0:T(8,128)(2,1)S(1)} %broadcast_in_dim.8), channel_id=1, replica_groups=mesh['y'=8,'x'=4,'core'=2,'space'=8] {'y','x'}, dimensions={0} | all-to-all | bytes 1835008 | tf_op jit(solution)/shard_map/all_to_all | solution.py:402
  35.5 4.8 %collective-permute-start = (bf16[32,112,128]{2,1,0:T(8,128)(2,1)S(1)}, bf16[32,112,128]{2,1,0:T(8,128)(2,1)S(1)}, u32[]{:S(2)}, u32[]{:S(2)}) collective-permute-start(bf16[32,112,128]{2,1,0:T(8,128)(2,1)S(1)} %all_to_all.25.mine), channel_id=1, source_target_pairs={{0,8},{8,0},{1,9},{9,1},{2,10},{10,2},{3,11},{11,3},{4,12},{12,4},... | collective-permute-start | bytes 2752520 | tf_op jit(solution)/shard_map/ppermute | solution.py:431
  40.3 0.0 copy-done.4
  40.3 0.9 broadcast_in_dim.10
  41.2 0.0 copy-start.5
  41.2 10.2 %all-to-all-start.1 = ((bf16[8,256,128]{2,1,0:T(8,128)(2,1)}), bf16[8,256,128]{2,1,0:T(8,128)(2,1)S(1)}, u32[]{:S(2)}, u32[]{:S(2)}) async-start(bf16[8,256,128]{2,1,0:T(8,128)(2,1)} %broadcast_in_dim.10), calls=%async_computation.1 | async-start | bytes 1048576 | tf_op jit(solution)/shard_map/all_to_all | solution.py:402
  51.4 0.1 pad_add_fusion.place
  51.4 0.0 copy-done.5
  51.4 29.1 %all_gather.3.image = bf16[2048,128]{1,0:T(8,128)(2,1)S(1)} all-gather(bf16[256,128]{1,0:T(8,128)(2,1)S(1)} %bitcast.9), channel_id=1, replica_groups=mesh['y'=8,'x'=4,'core'=2,'space'=8] {'space'}, dimensions={0}, use_global_device_ids=true | all-gather | bytes 589824 | tf_op jit(solution)/shard_map/all_gather | solution.py:430
  80.6 0.0 collective-permute-done.theirs
  80.6 6.2 %shard_map.75 = (f32[2048,128]{1,0:T(8,128)S(1)}, bf16[2048,128]{1,0:T(8,128)(2,1)S(1)}, f32[8,128]{1,0:T(8,128)S(1)}, bf16[3456,128]{1,0:T(8,128)(2,1)S(1)}) custom-call(s32[2]{0:T(128)S(1)} %pad_add_fusion.place, bf16[2048,128]{1,0:T(8,128)(2,1)S(1)} %all_gather.3.image, bf16[32,112,128]{2,1,0:T(8,128)(2,1)S(1)} %all_to_all.25.mine, ...), custom_call_target="tpu_custom_call" | custom-call | tf_op jit(solution)/shard_map/pallas_call | solution.py:307
  86.7 0.0 copy-start
  86.8 1.0 copy-done
  87.7 0.0 copy-start.2
  87.7 0.9 copy-done.2
  88.7 0.0 all-to-all-done.1
  88.7 0.0 copy-start.1
  88.7 12.7 %shard_map.76 = (bf16[256,128]{1,0:T(8,128)(2,1)}, f32[256,128]{1,0:T(8,128)S(1)}, bf16[2048,128]{1,0:T(8,128)(2,1)S(1)}, bf16[64,8,128]{2,1,0:T(8,128)(2,1)S(1)}, bf16[3456,128]{1,0:T(8,128)(2,1)S(1)}) custom-call(s32[2]{0:T(128)S(1)} %pad_add_fusion.place, bf16[2048,128]{1,0:T(8,128)(2,1)S(1)} %get-tuple-element.17.hidden, ...), custom_call_target="tpu_custom_call" | custom-call | tf_op jit(solution)/shard_map/pallas_call | solution.py:307
  101.3 0.0 copy-done.1
  101.3 12.6 %shard_map.77 = (bf16[2048,128]{1,0:T(8,128)(2,1)S(1)}, bf16[64,8,128]{2,1,0:T(8,128)(2,1)S(1)}) custom-call(s32[2]{0:T(128)S(1)} %pad_add_fusion.place, bf16[2048,128]{1,0:T(8,128)(2,1)S(1)} %get-tuple-element.19.second_delta, bf16[3456,128]{1,0:T(8,128)(2,1)S(1)} %get-tuple-element.20.weight, f32[2048,128]{1,0:T(8,128)S(1)} %copy-done.1, ...), custom_call_target="tpu_custom_call" | custom-call | tf_op jit(solution)/shard_map/pallas_call | solution.py:307
  113.9 0.0 copy-start.3
  113.9 22.6 %all_to_all.26.first = bf16[64,8,128]{2,1,0:T(8,128)(2,1)S(1)} all-to-all(bf16[64,8,128]{2,1,0:T(8,128)(2,1)S(1)} %get-tuple-element.26), channel_id=1, replica_groups=mesh['y'=8,'x'=4,'core'=2,'space'=8] {'y','x','core'}, dimensions={0} | all-to-all | bytes 262144 | tf_op jit(solution)/shard_map/all_to_all | solution.py:441
  136.5 14.9 %all_to_all.27.second = bf16[64,8,128]{2,1,0:T(8,128)(2,1)S(1)} all-to-all(bf16[64,8,128]{2,1,0:T(8,128)(2,1)S(1)} %get-tuple-element.27), channel_id=1, replica_groups=mesh['y'=8,'x'=4,'core'=2,'space'=8] {'y','x','core'}, dimensions={0} | all-to-all | bytes 262144 | tf_op jit(solution)/shard_map/all_to_all | solution.py:437
  151.4 0.1 shard_map.79
  151.5 0.6 broadcast_in_dim.22
  152.1 5.1 %all-to-all-start.4 = ((f32[8,16,128]{2,1,0:T(8,128)}), f32[8,16,128]{2,1,0:T(8,128)S(1)}, u32[]{:S(2)}, u32[]{:S(2)}) async-start(f32[8,16,128]{2,1,0:T(8,128)} %broadcast_in_dim.22), calls=%async_computation.4 | async-start | bytes 131072 | tf_op jit(solution)/shard_map/all_to_all | solution.py:402
  157.2 0.0 copy-done.3
  157.2 1.9 %shard_map.78 = bf16[256,128]{1,0:T(8,128)(2,1)} custom-call(s32[2]{0:T(128)S(1)} %pad_add_fusion.place, bf16[2048,128]{1,0:T(8,128)(2,1)S(1)} %get-tuple-element.23.delta, bf16[3456,128]{1,0:T(8,128)(2,1)S(1)} %copy-done.3, f32[256,128]{1,0:T(8,128)S(1)} %get-tuple-element.25.outer_slab), custom_call_target="tpu_custom_call" | custom-call | tf_op jit(solution)/shard_map/pallas_call | solution.py:307
  159.2 5.3 %all-to-all-done.4.pieces = f32[8,16,128]{2,1,0:T(8,128)S(1)} async-done(((f32[8,16,128]{2,1,0:T(8,128)}), f32[8,16,128]{2,1,0:T(8,128)S(1)}, u32[]{:S(2)}, u32[]{:S(2)}) %all-to-all-start.4) | async-done | bytes 65568 | tf_op jit(solution)/shard_map/all_to_all | solution.py:402
  164.4 0.6 shard_map.80
Async XLA Ops:
  1.5 38.8 %copy-start.4 = (bf16[1,4,8,8,128]{4,3,2,1,0:T(8,128)(2,1)S(1)}, bf16[1,4,8,8,128]{4,3,2,1,0:T(8,128)(2,1)}, u32[]{:S(2)}) copy-start(bf16[1,4,8,8,128]{4,3,2,1,0:T(8,128)(2,1)} %param.5) | copy-start | bytes 196612
  35.5 45.0 %collective-permute-start = (bf16[32,112,128]{2,1,0:T(8,128)(2,1)S(1)}, bf16[32,112,128]{2,1,0:T(8,128)(2,1)S(1)}, u32[]{:S(2)}, u32[]{:S(2)}) collective-permute-start(bf16[32,112,128]{2,1,0:T(8,128)(2,1)S(1)} %all_to_all.25.mine), channel_id=1, source_target_pairs={{0,8},{8,0},{1,9},{9,1},{2,10},{10,2},{3,11},{11,3},{4,12},{12,4},... | collective-permute-start | bytes 2752520 | tf_op jit(solution)/shard_map/ppermute | solution.py:431
  41.2 10.2 %copy-start.5 = (bf16[1,4,8,8,128]{4,3,2,1,0:T(8,128)(2,1)S(1)}, bf16[1,4,8,8,128]{4,3,2,1,0:T(8,128)(2,1)}, u32[]{:S(2)}) copy-start(bf16[1,4,8,8,128]{4,3,2,1,0:T(8,128)(2,1)} %param.4) | copy-start | bytes 196612
  41.2 47.5 %all-to-all-start.1 = ((bf16[8,256,128]{2,1,0:T(8,128)(2,1)}), bf16[8,256,128]{2,1,0:T(8,128)(2,1)S(1)}, u32[]{:S(2)}, u32[]{:S(2)}) async-start(bf16[8,256,128]{2,1,0:T(8,128)(2,1)} %broadcast_in_dim.10), calls=%async_computation.1 | async-start | bytes 1048576 | tf_op jit(solution)/shard_map/all_to_all | solution.py:402
  86.7 1.0 copy-start
  87.7 0.9 copy-start.2
  88.7 12.7 %copy-start.1 = (f32[2048,128]{1,0:T(8,128)S(1)}, f32[2048,128]{1,0:T(8,128)}, u32[]{:S(2)}) copy-start(f32[2048,128]{1,0:T(8,128)} %copy-done) | copy-start | bytes 3145732
  113.9 43.3 %copy-start.3 = (bf16[3456,128]{1,0:T(8,128)(2,1)S(1)}, bf16[3456,128]{1,0:T(8,128)(2,1)}, u32[]{:S(2)}) copy-start(bf16[3456,128]{1,0:T(8,128)(2,1)} %copy-done.2) | copy-start | bytes 2654212
  152.1 12.3 %all-to-all-start.4 = ((f32[8,16,128]{2,1,0:T(8,128)}), f32[8,16,128]{2,1,0:T(8,128)S(1)}, u32[]{:S(2)}, u32[]{:S(2)}) async-start(f32[8,16,128]{2,1,0:T(8,128)} %broadcast_in_dim.22), calls=%async_computation.4 | async-start | bytes 131072 | tf_op jit(solution)/shard_map/all_to_all | solution.py:402
